TPU v7x, 512 devices: a whole 4x8x8 slice. The times are simulated.
512 devices in a mesh: wide: 64 (over y, z), narrow: 8 (over x, core).
Axes of the slice: x: 4, y: 8, z: 8, core: 2. Of those that a mesh axis runs over, the one named last changes fastest.
Arguments:
- right_side: bfloat16 [4, 1024, 512], P(None, 'wide'), may hold values from -6 to 6
- partial_in: float32 [8, 4, 1024, 512], P('narrow', None, 'wide'), may hold values from -6 to 6
- window_factor: bfloat16 [4, 1024, 4, 1024], P(None, 'wide', None, 'narrow'), may hold values from -0.09375 to 0.09375
- inverse_t: bfloat16 [4, 1024, 1024], P(None, 'wide', 'narrow'), as said below
- trailing_factor: bfloat16 [131072, 4, 1024], P('wide', None, 'narrow'), may hold values from -0.09375 to 0.09375
Outputs:
- solved: bfloat16 [4, 1024, 512], P(None, 'narrow')
- trailing: float32 [131072, 512], P(('wide', 'narrow'))
Inputs may be any that keep to these rules, and one draw needn't show every extreme that they name: inverse_t[k] is the transpose of the inverse of the k-th diagonal block of the lower-triangular factor: entry [k, j, i] is zero where j > i.
All inputs are finite; a program needn't handle non-finite values.
Results may differ from a plain program's by a relative error of at most 0.012.
Values may be sent and summed in bfloat16 or wider, within the bound.
No kernel may reach another device: no remote copies, remote signals or barrier semaphores. Data moves between devices by JAX's collectives and lax.ppermute only.
A program may use at most 64 MiB of HBM per device.

v0:
```python
import jax
import jax.numpy as jnp
from jax import lax
from jax.sharding import PartitionSpec as P


def per_device(right_side, partial_in, window_factor, inverse_t, trailing_factor):
    steps_count = right_side.shape[0]
    col_width = inverse_t.shape[2]
    rhs_width = right_side.shape[2]
    trail_rows = trailing_factor.shape[0]
    solved_list = []
    for block in range(steps_count):
        fanned = partial_in[0, block]
        for prior in range(block):
            fanned = fanned + jnp.dot(
                window_factor[block, :, prior, :],
                solved_list[prior],
                preferred_element_type=jnp.float32,
            )
        fanned = lax.psum(fanned, "narrow")
        residue = (right_side[block].astype(jnp.float32) - fanned).astype(jnp.bfloat16)
        solution = lax.dot_general(
            lax.all_gather(inverse_t[block], "wide", axis=0, tiled=True),
            lax.all_gather(residue, "wide", axis=0, tiled=True),
            (((0,), (0,)), ((), ())),
            preferred_element_type=jnp.float32,
        )
        solution = solution.astype(jnp.bfloat16)
        solved_list.append(solution)
    solved = jnp.stack(solved_list)
    flat_factor = trailing_factor.reshape(trail_rows, steps_count * col_width)
    flat_solved = solved.reshape(steps_count * col_width, rhs_width)
    trailing = lax.psum_scatter(
        jnp.dot(flat_factor, flat_solved, preferred_element_type=jnp.float32),
        "narrow",
        scatter_dimension=0,
        tiled=True,
    )
    return (solved, trailing)


def solution(mesh):
    placed = (
        P(None, "wide", None),
        P("narrow", None, "wide", None),
        P(None, "wide", None, "narrow"),
        P(None, "wide", "narrow"),
        P("wide", None, "narrow"),
    )
    return jax.shard_map(
        per_device,
        mesh=mesh,
        in_specs=placed,
        out_specs=(P(None, "narrow", None), P(("wide", "narrow"), None)),
        check_vma=False,
    )
```

profile of v0, /device:TPU:8, one launch (start us, length us, event | category | flops | bytes accessed | tf_op | source)
XLA Modules:
  0.0 483.0 jit_solution(5871402175136502424)
XLA Ops:
  7.2 0.0 copy-start
  7.2 0.0 copy-start.1
  7.2 0.0 copy-start.2
  7.2 0.0 all-gather.9.cloned.1.call-start
  7.2 0.9 slice_bitcast_fusion
  8.2 25.6 %psum.28 = f32[16,512]{1,0:T(8,128)S(1)} all-reduce(f32[16,512]{1,0:T(8,128)S(1)} %slice_bitcast_fusion), channel_id=1, replica_groups=mesh['wide'=64,'narrow'=8] {'narrow'}, use_global_device_ids=true, to_apply=%region_0.0 | all-reduce | flops 8192 | bytes 65536 | tf_op jit(solution)/shard_map/psum | solution.py:21
  33.8 1.3 fusion.15
  35.1 0.0 all-gather.9.cloned.1.call-update
  35.1 0.0 all-gather.11.cloned.1.call-start
  35.2 0.7 fusion.17
  35.9 56.0 %all-gather = bf16[1,1024,128]{2,1,0:T(8,128)(2,1)S(1)} all-gather(bf16[1,16,128]{2,1,0:T(8,128)(2,1)S(1)} %get-tuple-element.14), channel_id=2, replica_groups=mesh['wide'=64,'narrow'=8] {'wide'}, dimensions={1}, use_global_device_ids=true | all-gather | bytes 266240 | tf_op jit(solution)/shard_map/all_gather | solution.py:24
  91.9 0.9 fusion.16
  92.8 26.1 %all-gather.9.cloned.1.call-done = bf16[1024,512]{1,0:T(8,128)(2,1)} async-done(((bf16[16,512]{1,0:T(8,128)(2,1)}), bf16[1024,512]{1,0:T(8,128)(2,1)}) %all-gather.9.cloned.1.call-update) | async-done | bytes 1048592 | tf_op jit(solution)/shard_map/all_gather | solution.py:25
  118.9 1.7 convolution_convert_fusion.3
  120.6 0.9 fusion.7
  121.5 23.6 %psum.29 = f32[16,512]{1,0:T(8,128)S(1)} all-reduce(f32[16,512]{1,0:T(8,128)S(1)} %fusion.7), channel_id=1, replica_groups=mesh['wide'=64,'narrow'=8] {'narrow'}, use_global_device_ids=true, to_apply=%region_1.0 | all-reduce | flops 8192 | bytes 65536 | tf_op jit(solution)/shard_map/psum | solution.py:21
  145.1 0.0 copy-done.2
  145.1 0.6 fusion.14
  145.7 0.0 all-gather.11.cloned.1.call-update
  145.7 0.0 all-gather.13.cloned.1.call-start
  145.8 48.2 %all-gather.1 = bf16[1,1024,128]{2,1,0:T(8,128)(2,1)S(1)} all-gather(bf16[1,16,128]{2,1,0:T(8,128)(2,1)S(1)} %get-tuple-element.13), channel_id=3, replica_groups=mesh['wide'=64,'narrow'=8] {'wide'}, dimensions={1}, use_global_device_ids=true | all-gather | bytes 266240 | tf_op jit(solution)/shard_map/all_gather | solution.py:24
  194.0 0.1 fusion.6
  194.2 28.4 %all-gather.11.cloned.1.call-done = bf16[1024,512]{1,0:T(8,128)(2,1)} async-done(((bf16[16,512]{1,0:T(8,128)(2,1)}), bf16[1024,512]{1,0:T(8,128)(2,1)}) %all-gather.11.cloned.1.call-update) | async-done | bytes 1048592 | tf_op jit(solution)/shard_map/all_gather | solution.py:25
  222.6 1.7 convolution_convert_fusion.2
  224.3 0.1 fusion.5
  224.4 23.6 %psum.30 = f32[16,512]{1,0:T(8,128)S(1)} all-reduce(f32[16,512]{1,0:T(8,128)S(1)} %fusion.5), channel_id=1, replica_groups=mesh['wide'=64,'narrow'=8] {'narrow'}, use_global_device_ids=true, to_apply=%region_2.0 | all-reduce | flops 8192 | bytes 65536 | tf_op jit(solution)/shard_map/psum | solution.py:21
  248.0 0.6 fusion.13
  248.6 0.0 all-gather.13.cloned.1.call-update
  248.7 0.0 all-gather.15.cloned.1.call-start
  248.7 48.2 %all-gather.2 = bf16[1,1024,128]{2,1,0:T(8,128)(2,1)S(1)} all-gather(bf16[1,16,128]{2,1,0:T(8,128)(2,1)S(1)} %get-tuple-element.15), channel_id=4, replica_groups=mesh['wide'=64,'narrow'=8] {'wide'}, dimensions={1}, use_global_device_ids=true | all-gather | bytes 266240 | tf_op jit(solution)/shard_map/all_gather | solution.py:24
  296.9 0.2 fusion.4
  297.1 0.1 fusion.3
  297.2 28.3 %all-gather.13.cloned.1.call-done = bf16[1024,512]{1,0:T(8,128)(2,1)} async-done(((bf16[16,512]{1,0:T(8,128)(2,1)}), bf16[1024,512]{1,0:T(8,128)(2,1)}) %all-gather.13.cloned.1.call-update) | async-done | bytes 1048592 | tf_op jit(solution)/shard_map/all_gather | solution.py:25
  325.5 1.7 convolution_convert_fusion.1
  327.2 0.1 fusion.2
  327.4 23.6 %psum.31 = f32[16,512]{1,0:T(8,128)S(1)} all-reduce(f32[16,512]{1,0:T(8,128)S(1)} %fusion.2), channel_id=1, replica_groups=mesh['wide'=64,'narrow'=8] {'narrow'}, use_global_device_ids=true, to_apply=%region_3.0 | all-reduce | flops 8192 | bytes 65536 | tf_op jit(solution)/shard_map/psum | solution.py:21
  351.0 0.6 fusion.12
  351.6 0.0 all-gather.15.cloned.1.call-update
  351.6 0.0 reduce-scatter.2.cloned.1.call-start
  351.7 48.2 %all-gather.3 = bf16[1,1024,128]{2,1,0:T(8,128)(2,1)S(1)} all-gather(bf16[1,16,128]{2,1,0:T(8,128)(2,1)S(1)} %get-tuple-element.12), channel_id=5, replica_groups=mesh['wide'=64,'narrow'=8] {'wide'}, dimensions={1}, use_global_device_ids=true | all-gather | bytes 266240 | tf_op jit(solution)/shard_map/all_gather | solution.py:24
  399.9 28.6 %all-gather.15.cloned.1.call-done = bf16[1024,512]{1,0:T(8,128)(2,1)} async-done(((bf16[16,512]{1,0:T(8,128)(2,1)}), bf16[1024,512]{1,0:T(8,128)(2,1)}) %all-gather.15.cloned.1.call-update) | async-done | bytes 1048592 | tf_op jit(solution)/shard_map/all_gather | solution.py:25
  428.5 1.7 fusion.1
  430.2 3.2 convolution_bitcast_fusion
  433.4 0.0 reduce-scatter.2.cloned.1.call-update
  433.4 0.1 pad_maximum_fusion
  433.5 1.0 copy.17
  434.5 39.9 %reduce-scatter.2.cloned.1.call-done = f32[256,512]{0,1:T(8,128)} async-done(((f32[2048,512]{0,1:T(8,128)}), f32[256,512]{0,1:T(8,128)}) %reduce-scatter.2.cloned.1.call-update) | async-done | bytes 524304 | tf_op jit(solution)/shard_map/reduce_scatter | solution.py:34
  474.5 2.0 copy.18
  (2 shorter events, 0.0 us)
Async XLA Ops:
  7.2 423.0 %copy-start = (bf16[2048,4,128]{2,1,0:T(4,128)(2,1)S(1)}, bf16[2048,4,128]{2,1,0:T(4,128)(2,1)}, u32[]{:S(2)}) copy-start(bf16[2048,4,128]{2,1,0:T(4,128)(2,1)} %param.9) | copy-start | bytes 6291460
  7.2 186.8 %copy-start.1 = (f32[1,4,16,512]{3,2,1,0:T(8,128)S(1)}, f32[1,4,16,512]{3,2,1,0:T(8,128)}, u32[]{:S(2)}) copy-start(f32[1,4,16,512]{3,2,1,0:T(8,128)} %param.6) | copy-start | bytes 393220
  7.2 137.9 %copy-start.2 = (bf16[4,16,512]{2,1,0:T(8,128)(2,1)S(1)}, bf16[4,16,512]{2,1,0:T(8,128)(2,1)}, u32[]{:S(2)}) copy-start(bf16[4,16,512]{2,1,0:T(8,128)(2,1)} %param.5) | copy-start | bytes 196612
  7.2 111.7 %all-gather.9.cloned.1.call-start = ((), (), s32[]{:S(2)}) async-start(), calls=%async_computation.1 | async-start | bytes 1064960 | tf_op jit(solution)/shard_map/all_gather | solution.py:25
  35.1 187.4 %all-gather.11.cloned.1.call-start = ((), (), s32[]{:S(2)}) async-start(), calls=%async_computation.2 | async-start | bytes 1064960 | tf_op jit(solution)/shard_map/all_gather | solution.py:25
  145.7 179.8 %all-gather.13.cloned.1.call-start = ((), (), s32[]{:S(2)}) async-start(), calls=%async_computation.3 | async-start | bytes 1064960 | tf_op jit(solution)/shard_map/all_gather | solution.py:25
  248.7 179.8 %all-gather.15.cloned.1.call-start = ((), (), s32[]{:S(2)}) async-start(), calls=%async_computation.4 | async-start | bytes 1064960 | tf_op jit(solution)/shard_map/all_gather | solution.py:25
  351.6 122.8 %reduce-scatter.2.cloned.1.call-start = ((), (), s32[]{:S(2)}) async-start(), calls=%async_computation.5 | async-start | bytes 4718592 | tf_op jit(solution)/shard_map/reduce_scatter | solution.py:34
Sparse Core Ops, SparseCore 0:
  35.2 83.6 all-gather.8
  145.9 76.6 all-gather.10
  248.8 76.6 all-gather.12
  351.7 76.6 all-gather.14
  433.6 40.8 reduce-scatter.1
where the time goes:
time: 484 us; the launch traced here: 483 us
  blocking collectives  297 us (61%)
  waiting for transfers between devices  151 us (31%)
  between operations  13.9 us (3%)
  matrix products  11.7 us (2%)
  local copies, waits for them, and re-layouts  5.6 us (1%)
    all_gather x4, blocking collectives, per_device(): lax.all_gather(inverse_t[block], 'wide', axis=0, tiled=True)  201 us
    all_gather x4, waiting for transfers between devices, per_device(): lax.all_gather(residue, 'wide', axis=0, tiled=True)  111 us
    psum x4, blocking collectives, per_device(): fanned = lax.psum(fanned, 'narrow')  96.4 us
    reduce_scatter x1, waiting for transfers between devices, per_device(): lax.psum_scatter(jnp.dot(flat_factor, flat_solved, preferred_element_type...  39.9 us
  transfers between devices with their start and end apart: 5, of which 5 were waited for; matrix products, arithmetic and copies ran while one was open for 1% of the time, Pallas kernels for 0%

commit v1 on v0

--- a/solution.py
+++ b/solution.py
@@ -18,7 +18,7 @@
                 solved_list[prior],
                 preferred_element_type=jnp.float32,
             )
-        fanned = lax.psum(fanned, "narrow")
+        fanned = jnp.sum(lax.all_gather(fanned, "narrow"), axis=0)
         residue = (right_side[block].astype(jnp.float32) - fanned).astype(jnp.bfloat16)
         solution = lax.dot_general(
             lax.all_gather(inverse_t[block], "wide", axis=0, tiled=True),

time: 484 us -> 446 us (0.921)
  blocking collectives: 297 us -> 253 us
  waiting for transfers between devices: 151 us -> 158 us
    psum x4 -> x0, blocking collectives: 96.4 us -> none  [per_device(): fanned = lax.psum(fanned, 'narrow')]
    all_gather x0 -> x4, blocking collectives: none -> 52.6 us  [per_device(): fanned = jnp.sum(lax.all_gather(fanned, 'narrow'), axis=0)]
    all_gather x4, waiting for transfers between devices: 111 us -> 118 us  [per_device(): lax.all_gather(residue, 'wide', axis=0, tiled=True)]
where the time goes in v1:
time: 446 us
  blocking collectives  253 us (57%)
  waiting for transfers between devices  158 us (35%)
  between operations  13.9 us (3%)
  matrix products  10.9 us (2%)
  local copies, waits for them, and re-layouts  5.59 us (1%)
    all_gather x4, blocking collectives, per_device(): lax.all_gather(inverse_t[block], 'wide', axis=0, tiled=True)  201 us
    all_gather x4, waiting for transfers between devices, per_device(): lax.all_gather(residue, 'wide', axis=0, tiled=True)  118 us
    all_gather x4, blocking collectives, per_device(): fanned = jnp.sum(lax.all_gather(fanned, 'narrow'), axis=0)  52.6 us
    reduce_scatter x1, waiting for transfers between devices, per_device(): lax.psum_scatter(jnp.dot(flat_factor, flat_solved, preferred_element_type...  39.8 us
  transfers between devices with their start and end apart: 5, of which 5 were waited for; matrix products, arithmetic and copies ran while one was open for 1% of the time, Pallas kernels for 0%

profile of v1, /device:TPU:8, one launch (start us, length us, event | category | flops | bytes accessed | tf_op | source)
XLA Modules:
  0.0 445.7 jit_solution(13131205314668911513)
XLA Ops:
  7.2 0.0 copy-start
  7.2 0.0 copy-start.1
  7.2 0.0 copy-start.2
  7.2 0.0 all-gather.13.cloned.1.call-start
  7.2 0.9 slice.55
  8.2 13.2 %all-gather = f32[8,1,16,512]{3,2,1,0:T(8,128)S(1)} all-gather(f32[1,1,16,512]{3,2,1,0:T(8,128)S(1)} %slice.55), channel_id=2, replica_groups=mesh['wide'=64,'narrow'=8] {'narrow'}, dimensions={0}, use_global_device_ids=true | all-gather | bytes 294912 | tf_op jit(solution)/shard_map/all_gather | solution.py:21
  21.3 1.3 fusion.15
  22.7 0.0 all-gather.13.cloned.1.call-update
  22.7 0.0 all-gather.15.cloned.1.call-start
  22.8 0.7 fusion.17
  23.5 56.0 %all-gather.1 = bf16[1,1024,128]{2,1,0:T(8,128)(2,1)S(1)} all-gather(bf16[1,16,128]{2,1,0:T(8,128)(2,1)S(1)} %get-tuple-element.16), channel_id=3, replica_groups=mesh['wide'=64,'narrow'=8] {'wide'}, dimensions={1}, use_global_device_ids=true | all-gather | bytes 266240 | tf_op jit(solution)/shard_map/all_gather | solution.py:24
  79.5 0.9 fusion.16
  80.4 28.0 %all-gather.13.cloned.1.call-done = bf16[1024,512]{1,0:T(8,128)(2,1)} async-done(((bf16[16,512]{1,0:T(8,128)(2,1)}), bf16[1024,512]{1,0:T(8,128)(2,1)}) %all-gather.13.cloned.1.call-update) | async-done | bytes 1048592 | tf_op jit(solution)/shard_map/all_gather | solution.py:25
  108.3 1.7 convolution_convert_fusion.3
  110.0 0.1 fusion.7
  110.2 13.1 %all-gather.2 = f32[128,512]{1,0:T(8,128)S(1)} all-gather(f32[16,512]{1,0:T(8,128)S(1)} %fusion.7), channel_id=4, replica_groups=mesh['wide'=64,'narrow'=8] {'narrow'}, dimensions={0}, use_global_device_ids=true | all-gather | bytes 294912 | tf_op jit(solution)/shard_map/all_gather | solution.py:21
  123.4 0.6 fusion.14
  124.0 0.0 all-gather.15.cloned.1.call-update
  124.0 0.0 all-gather.17.cloned.1.call-start
  124.0 48.3 %all-gather.3 = bf16[1,1024,128]{2,1,0:T(8,128)(2,1)S(1)} all-gather(bf16[1,16,128]{2,1,0:T(8,128)(2,1)S(1)} %get-tuple-element.15), channel_id=5, replica_groups=mesh['wide'=64,'narrow'=8] {'wide'}, dimensions={1}, use_global_device_ids=true | all-gather | bytes 266240 | tf_op jit(solution)/shard_map/all_gather | solution.py:24
  172.3 0.1 fusion.6
  172.5 30.2 %all-gather.15.cloned.1.call-done = bf16[1024,512]{1,0:T(8,128)(2,1)} async-done(((bf16[16,512]{1,0:T(8,128)(2,1)}), bf16[1024,512]{1,0:T(8,128)(2,1)}) %all-gather.15.cloned.1.call-update) | async-done | bytes 1048592 | tf_op jit(solution)/shard_map/all_gather | solution.py:25
  202.6 1.7 convolution_convert_fusion.2
  204.3 0.1 fusion.5
  204.5 13.1 %all-gather.4 = f32[128,512]{1,0:T(8,128)S(1)} all-gather(f32[16,512]{1,0:T(8,128)S(1)} %fusion.5), channel_id=6, replica_groups=mesh['wide'=64,'narrow'=8] {'narrow'}, dimensions={0}, use_global_device_ids=true | all-gather | bytes 294912 | tf_op jit(solution)/shard_map/all_gather | solution.py:21
  217.6 0.6 fusion.13
  218.3 0.0 all-gather.17.cloned.1.call-update
  218.3 0.0 all-gather.19.cloned.1.call-start
  218.3 48.3 %all-gather.5 = bf16[1,1024,128]{2,1,0:T(8,128)(2,1)S(1)} all-gather(bf16[1,16,128]{2,1,0:T(8,128)(2,1)S(1)} %get-tuple-element.17), channel_id=7, replica_groups=mesh['wide'=64,'narrow'=8] {'wide'}, dimensions={1}, use_global_device_ids=true | all-gather | bytes 266240 | tf_op jit(solution)/shard_map/all_gather | solution.py:24
  266.6 0.1 fusion.4
  266.8 0.2 fusion.3
  266.9 30.0 %all-gather.17.cloned.1.call-done = bf16[1024,512]{1,0:T(8,128)(2,1)} async-done(((bf16[16,512]{1,0:T(8,128)(2,1)}), bf16[1024,512]{1,0:T(8,128)(2,1)}) %all-gather.17.cloned.1.call-update) | async-done | bytes 1048592 | tf_op jit(solution)/shard_map/all_gather | solution.py:25
  296.9 1.7 convolution_convert_fusion.1
  298.6 0.1 fusion.2
  298.8 13.1 %all-gather.6 = f32[128,512]{1,0:T(8,128)S(1)} all-gather(f32[16,512]{1,0:T(8,128)S(1)} %fusion.2), channel_id=8, replica_groups=mesh['wide'=64,'narrow'=8] {'narrow'}, dimensions={0}, use_global_device_ids=true | all-gather | bytes 294912 | tf_op jit(solution)/shard_map/all_gather | solution.py:21
  311.9 0.6 fusion.12
  312.5 0.0 all-gather.19.cloned.1.call-update
  312.6 0.0 reduce-scatter.2.cloned.1.call-start
  312.6 48.3 %all-gather.7 = bf16[1,1024,128]{2,1,0:T(8,128)(2,1)S(1)} all-gather(bf16[1,16,128]{2,1,0:T(8,128)(2,1)S(1)} %get-tuple-element.14), channel_id=9, replica_groups=mesh['wide'=64,'narrow'=8] {'wide'}, dimensions={1}, use_global_device_ids=true | all-gather | bytes 266240 | tf_op jit(solution)/shard_map/all_gather | solution.py:24
  360.9 30.3 %all-gather.19.cloned.1.call-done = bf16[1024,512]{1,0:T(8,128)(2,1)} async-done(((bf16[16,512]{1,0:T(8,128)(2,1)}), bf16[1024,512]{1,0:T(8,128)(2,1)}) %all-gather.19.cloned.1.call-update) | async-done | bytes 1048592 | tf_op jit(solution)/shard_map/all_gather | solution.py:25
  391.2 1.7 fusion.1
  392.9 0.0 copy-done
  392.9 3.2 convolution_bitcast_fusion
  396.1 0.0 reduce-scatter.2.cloned.1.call-update
  396.2 0.1 pad_maximum_fusion
  396.2 1.0 copy.26
  397.3 39.8 %reduce-scatter.2.cloned.1.call-done = f32[256,512]{0,1:T(8,128)} async-done(((f32[2048,512]{0,1:T(8,128)}), f32[256,512]{0,1:T(8,128)}) %reduce-scatter.2.cloned.1.call-update) | async-done | bytes 524304 | tf_op jit(solution)/shard_map/reduce_scatter | solution.py:34
  437.1 2.0 copy.27
  (6 shorter events, 0.1 us)
Async XLA Ops:
  7.2 385.7 %copy-start = (bf16[2048,4,128]{2,1,0:T(4,128)(2,1)S(1)}, bf16[2048,4,128]{2,1,0:T(4,128)(2,1)}, u32[]{:S(2)}) copy-start(bf16[2048,4,128]{2,1,0:T(4,128)(2,1)} %param.9) | copy-start | bytes 6291460
  7.2 102.9 %copy-start.1 = (f32[1,4,16,512]{3,2,1,0:T(8,128)S(1)}, f32[1,4,16,512]{3,2,1,0:T(8,128)}, u32[]{:S(2)}) copy-start(f32[1,4,16,512]{3,2,1,0:T(8,128)} %param.6) | copy-start | bytes 393220
  7.2 116.2 %copy-start.2 = (bf16[4,16,512]{2,1,0:T(8,128)(2,1)S(1)}, bf16[4,16,512]{2,1,0:T(8,128)(2,1)}, u32[]{:S(2)}) copy-start(bf16[4,16,512]{2,1,0:T(8,128)(2,1)} %param.5) | copy-start | bytes 196612
  7.2 101.1 %all-gather.13.cloned.1.call-start = ((), (), s32[]{:S(2)}) async-start(), calls=%async_computation.1 | async-start | bytes 1064960 | tf_op jit(solution)/shard_map/all_gather | solution.py:25
  22.7 179.9 %all-gather.15.cloned.1.call-start = ((), (), s32[]{:S(2)}) async-start(), calls=%async_computation.2 | async-start | bytes 1064960 | tf_op jit(solution)/shard_map/all_gather | solution.py:25
  124.0 172.9 %all-gather.17.cloned.1.call-start = ((), (), s32[]{:S(2)}) async-start(), calls=%async_computation.3 | async-start | bytes 1064960 | tf_op jit(solution)/shard_map/all_gather | solution.py:25
  218.3 172.9 %all-gather.19.cloned.1.call-start = ((), (), s32[]{:S(2)}) async-start(), calls=%async_computation.4 | async-start | bytes 1064960 | tf_op jit(solution)/shard_map/all_gather | solution.py:25
  312.6 124.5 %reduce-scatter.2.cloned.1.call-start = ((), (), s32[]{:S(2)}) async-start(), calls=%async_computation.5 | async-start | bytes 4718592 | tf_op jit(solution)/shard_map/reduce_scatter | solution.py:34
Sparse Core Ops, SparseCore 0:
  22.8 85.4 all-gather.12
  124.1 78.4 all-gather.14
  218.4 78.4 all-gather.16
  312.7 78.4 all-gather.18
  396.3 40.7 reduce-scatter.1
